TPU v7x, 32 devices: a whole 2x2x4 slice. The times are simulated.
32 devices in a mesh: section: 4 (over y, core), space: 8 (over z, x).
Axes of the slice: x: 2, y: 2, z: 4, core: 2. Of those that a mesh axis runs over, the one named last changes fastest.
Arguments:
- features: bfloat16 [4, 2048, 256], P('section', 'space'), may hold values from -6 to 6
- out_grad: bfloat16 [4, 2048, 256], P('section', 'space'), may hold values from -6 to 6
- weight: bfloat16 [4, 27, 256, 256], P('section'), may hold values from -0.078125 to 0.078125
- counts: int32 [4, 16], P('section', 'space'), may hold values from 16 to 128
- local_rows: int32 [4, 27, 2048], P('section', None, 'space'), may hold values from -1 to 255, as said below
- send_rows: int32 [4, 8, 27, 8, 2], P('section', 'space'), may hold values from -1 to 255, as said below
- recv_rows: int32 [4, 8, 27, 8, 2], P('section', 'space'), may hold values from -1 to 255, as said below
Outputs:
- handoff: bfloat16 [4, 2048, 256], P('section', 'space')
- weight_grad: float32 [4, 6912, 256], P('section', 'space')
Inputs may be any that keep to these rules, and one draw needn't show every extreme that they name: `local_rows`: -1 where a voxel has no pair on its own device at that offset. `send_rows`: for each offset and two different devices, the first 1 to 2 slots are used and the rest are -1; a device's slots to itself are all -1; for every sending device there is one offset at which all 2 slots to every other device are used. `recv_rows`: slot for slot the pairs of send_rows seen from the receiving device, -1 in the same empty slots.
All inputs are finite; a program needn't handle non-finite values.
Results may differ from a plain program's by a relative error of at most 0.0019.
Values may be sent and summed in bfloat16 or wider, within the bound.
No kernel may reach another device: no remote copies, remote signals or barrier semaphores. Data moves between devices by JAX's collectives and lax.ppermute only.
A program may use at most 64 MiB of HBM per device.

v0:
```python
import jax
import jax.numpy as jnp
from jax import lax
from jax.sharding import PartitionSpec as P

BLOCK = 128


def from_behind(block, axis, distance):
    devices = range(lax.axis_size(axis))
    route = [(i - distance, i) for i in devices if i - distance in devices]
    return lax.ppermute(block, axis, route)


def take_rows(source, row_index, nothing):
    picked = jnp.take(source, jnp.maximum(row_index, 0), axis=0)
    return jnp.where((row_index >= 0)[..., None], picked, nothing)


def body(features, out_grad, weight, counts, local_rows, send_rows, recv_rows):
    inputs = features[0]
    gradient = out_grad[0]
    kernel = weight[0]
    rows_dev = inputs.shape[0]
    channels = inputs.shape[1]
    offsets = kernel.shape[0]
    inside = (jnp.arange(BLOCK, dtype=jnp.int32)[None, :] < counts[0][:, None]).reshape(rows_dev, 1)
    nothing = jnp.zeros((), inputs.dtype)
    xmask = jnp.where(inside, inputs, nothing)
    gmask = jnp.where(inside, gradient, nothing)
    local_map = local_rows[0].T
    gathered = take_rows(gmask, local_map, nothing)
    input_grad = lax.dot_general(
        gathered, kernel, (((1, 2), (0, 1)), ((), ())), preferred_element_type=jnp.float32
    )
    weight_grad = lax.dot_general(
        gathered, xmask, (((0,), (0,)), ((), ())), preferred_element_type=jnp.float32
    )
    send_map = send_rows[0, 0]
    recv_map = recv_rows[0, 0]
    flat_shape = (offsets, -1, channels)
    outgoing = take_rows(gmask, send_map, nothing)
    partial_value = (
        lax.dot_general(
            outgoing.reshape(flat_shape),
            kernel,
            (((2,), (1,)), ((0,), (0,))),
            preferred_element_type=jnp.float32,
        )
        .astype(jnp.bfloat16)
        .reshape(outgoing.shape)
    )
    arrived = lax.all_to_all(partial_value, "space", split_axis=1, concat_axis=1, tiled=True)
    returned = lax.all_to_all(
        take_rows(xmask, recv_map, nothing), "space", split_axis=1, concat_axis=1, tiled=True
    )
    weight_grad = weight_grad + lax.dot_general(
        outgoing.reshape(flat_shape),
        returned.reshape(flat_shape),
        (((1,), (1,)), ((0,), (0,))),
        preferred_element_type=jnp.float32,
    )
    incoming = arrived.reshape(-1, channels).astype(jnp.float32)
    target = jnp.where(recv_map >= 0, recv_map, rows_dev).reshape(-1)
    input_grad = input_grad.at[target].add(incoming, mode="drop")
    result = jnp.where(inside, input_grad, 0.0).astype(jnp.bfloat16)
    handoff = from_behind(result, "section", -1)
    loss_scale = float(rows_dev * lax.axis_size("space")) ** (-0.5)
    summed = lax.psum_scatter(
        (weight_grad * loss_scale).reshape(offsets * channels, channels),
        "space",
        scatter_dimension=0,
        tiled=True,
    )
    return (handoff[None], summed[None])


def solution(mesh):
    placed = (
        P("section", "space", None),
        P("section", "space", None),
        P("section", None, None, None),
        P("section", "space"),
        P("section", None, "space"),
        P("section", "space", None, None, None),
        P("section", "space", None, None, None),
    )
    return jax.shard_map(
        body,
        mesh=mesh,
        in_specs=placed,
        out_specs=(P("section", "space", None), P("section", "space", None)),
        check_vma=False,
    )
```

profile of v0, /device:TPU:0, one launch (start us, length us, event | category | flops | bytes accessed | tf_op | source)
XLA Modules:
  0.0 275.7 jit_solution(11968080390307770625)
XLA Ops:
  15.3 3.1 %gather_fusion.1 = bf16[432,256]{1,0:T(8,128)(2,1)} fusion(bf16[256,256]{1,0:T(8,128)(2,1)} %bitcast_select_fusion.1, s32[1024]{0:T(1024)S(1)} %pad_clamp_fusion.2), kind=kCustom, calls=%fused_computation.clone | custom fusion | bytes 444096 | tf_op jit(solution)/shard_map/jit(_take)/gather | solution.py:16
  18.4 1.7 reshape.145
  20.1 2.3 broadcast_select_fusion.3
  25.0 2.2 fusion.4
  27.2 1.7 reshape.100
  28.9 1.8 copy.90
  30.7 7.3 %all-to-all-start = ((bf16[27,8,2,256]{3,2,0,1:T(2,128)(2,1)}), bf16[27,8,2,256]{3,2,0,1:T(2,128)(2,1)}, u32[]{:S(2)}, u32[]{:S(2)}) async-start(bf16[27,8,2,256]{3,2,0,1:T(2,128)(2,1)} %copy.90), calls=%async_computation | async-start | bytes 442368 | tf_op jit(solution)/shard_map/all_to_all | solution.py:53
  48.8 1.7 reshape.122
  55.4 18.5 %gather_fusion = bf16[6912,256]{1,0:T(8,128)(2,1)} fusion(bf16[256,256]{1,0:T(8,128)(2,1)} %bitcast_select_fusion.1, s32[7168]{0:T(1024)} %pad_clamp_fusion), kind=kCustom, calls=%fused_computation.2 | custom fusion | bytes 7105536 | tf_op jit(solution)/shard_map/jit(_take)/gather | solution.py:16
  73.9 6.4 %reshape.121 = bf16[256,27,256]{2,1,0:T(8,128)(2,1)} reshape(bf16[6912,256]{1,0:T(8,128)(2,1)} %gather_fusion) | data formatting | bytes 7077888 | tf_op jit(solution)/shard_map/jit(_take)/gather | solution.py:16
  80.3 7.6 %select_select_fusion = bf16[256,27,256]{2,1,0:T(8,128)(2,1)} fusion(bf16[256,27,256]{2,1,0:T(8,128)(2,1)} %reshape.121, pred[256,27]{1,0:T(8,128)(4,1)} %copy.81, pred[256,27]{1,0:T(8,128)(4,1)} %bitcast.53), kind=kLoop, calls=%fused_computation.5 | loop fusion | flops 3538944 | bytes 7091712 | tf_op jit(solution)/shard_map/jit(_where)/select_n | solution.py:17
  87.9 7.4 %copy.93 = bf16[256,27,256]{0,2,1:T(8,128)(2,1)} copy(bf16[256,27,256]{2,1,0:T(8,128)(2,1)} %select_select_fusion) | data formatting | bytes 7077888 | tf_op jit(solution)/shard_map/jit(_where)/select_n | solution.py:17
  95.3 3.8 %fusion.7 = f32[256,256]{1,0:T(8,128)} fusion(bf16[256,27,256]{0,2,1:T(8,128)(2,1)} %copy.93, bf16[1,27,256,256]{3,2,1,0:T(8,128)(2,1)S(1)} %copy-done), kind=kOutput, calls=%fused_computation.11 | convolution fusion | flops 905969664 | bytes 7340032 | tf_op jit(solution)/shard_map/dot_general | solution.py:33
  101.1 2.1 reshape.132
  103.1 4.7 %scatter_fusion = f32[256,256]{1,0:T(8,128)} fusion(f32[256,256]{1,0:T(8,128)} %fusion.7, s32[432]{0:T(512)S(1)} %bitcast.54, f32[432,256]{1,0:T(8,128)} %reshape.132), kind=kCustom, calls=%fused_computation.3 | custom fusion | flops 110592 | bytes 1328832 | tf_op jit(solution)/shard_map/scatter-add | solution.py:65
  107.9 1.8 bitcast_select_fusion
  109.7 3.1 %gather_fusion.2 = bf16[432,256]{1,0:T(8,128)(2,1)} fusion(bf16[256,256]{1,0:T(8,128)(2,1)} %get-tuple-element.7, s32[1024]{0:T(1024)S(1)} %pad_clamp_fusion.1), kind=kCustom, calls=%fused_computation.1.clone | custom fusion | bytes 444096 | tf_op jit(solution)/shard_map/jit(_take)/gather | solution.py:16
  112.8 1.7 reshape.149
  114.5 2.3 broadcast_select_fusion.2
  116.8 13.7 %all_to_all.10 = bf16[27,8,2,256]{3,2,0,1:T(2,128)(2,1)S(1)} all-to-all(bf16[27,8,2,256]{3,2,0,1:T(2,128)(2,1)S(1)} %broadcast_select_fusion.2), channel_id=1, replica_groups=mesh['section'=4,'space'=8] {'space'}, dimensions={1} | all-to-all | bytes 442368 | tf_op jit(solution)/shard_map/all_to_all | solution.py:54
  133.1 2.3 fusion.11
  135.4 4.0 %add_multiply_fusion = f32[27,256,256]{2,1,0:T(8,128)} fusion(f32[27,256,256]{2,1,0:T(8,128)S(1)} %fusion.11, bf16[256,27,256]{0,2,1:T(8,128)(2,1)S(1)} %copy-done.1, bf16[256,256]{1,0:T(8,128)(2,1)S(1)} %copy-done.2), kind=kOutput, calls=%fused_computation.4 | convolution fusion | flops 909508608 | bytes 17825792 | tf_op jit(solution)/shard_map/dot_general | solution.py:36
  140.7 2.3 collective-permute-done
  143.0 124.3 %reduce-scatter.2.cloned.1.call-done = f32[864,256]{1,0:T(8,128)} async-done(((f32[6912,256]{1,0:T(8,128)}), f32[864,256]{1,0:T(8,128)}) %reduce-scatter.2.cloned.1.call-update) | async-done | bytes 884752 | tf_op jit(solution)/shard_map/reduce_scatter | solution.py:69
  (49 shorter events, 33.7 us)
Async XLA Ops:
  7.2 17.8 %copy-start = (bf16[1,27,256,256]{3,2,1,0:T(8,128)(2,1)S(1)}, bf16[1,27,256,256]{3,2,1,0:T(8,128)(2,1)}, u32[]{:S(2)}) copy-start(bf16[1,27,256,256]{3,2,1,0:T(8,128)(2,1)} %param.11) | copy-start | bytes 10616836
  18.4 19.6 %copy-start.4 = (s32[1,1,27,8,2]{2,4,3,1,0:T(2,128)S(1)}, s32[1,1,27,8,2]{2,4,3,1,0:T(2,128)}, u32[]{:S(2)}) copy-start(s32[1,1,27,8,2]{2,4,3,1,0:T(2,128)} %param.15) | copy-start | bytes 5188
  30.7 68.4 %all-to-all-start = ((bf16[27,8,2,256]{3,2,0,1:T(2,128)(2,1)}), bf16[27,8,2,256]{3,2,0,1:T(2,128)(2,1)}, u32[]{:S(2)}, u32[]{:S(2)}) async-start(bf16[27,8,2,256]{3,2,0,1:T(2,128)(2,1)} %copy.90), calls=%async_computation | async-start | bytes 442368 | tf_op jit(solution)/shard_map/all_to_all | solution.py:53
  38.0 229.4 %reduce-scatter.2.cloned.1.call-start = ((), (), s32[]{:S(2)}) async-start(), calls=%async_computation.3 | async-start | bytes 7962624 | tf_op jit(solution)/shard_map/reduce_scatter | solution.py:69
  40.0 1.4 copy-start.3
  103.1 4.7 %copy-start.5 = (pred[256]{0:T(512)(128)(4,1)S(1)}, pred[256]{0:T(512)(128)(4,1)}, u32[]{:S(2)}) copy-start(pred[256]{0:T(512)(128)(4,1)} %compare_bitcast_fusion.2) | copy-start | bytes 772
  133.1 2.3 copy-start.1
  133.1 2.3 copy-start.2
  139.4 3.6 %collective-permute-start = (bf16[256,256]{1,0:T(8,128)(2,1)}, bf16[256,256]{1,0:T(8,128)(2,1)}, u32[]{:S(2)}, u32[]{:S(2)}) collective-permute-start(bf16[256,256]{1,0:T(8,128)(2,1)} %get-tuple-element.8), channel_id=1, source_target_pairs={{8,0},{16,8},{24,16},{9,1},{17,9},{25,17},{10,2},{18,10},{26,18},{... | collective-permute-start | bytes 393224 | tf_op jit(solution)/shard_map/ppermute | solution.py:12
Sparse Core Ops, SparseCore 0:
  139.6 127.7 reduce-scatter.1
where the time goes:
time: 278 us; the launch traced here: 276 us
  waiting for transfers between devices  127 us (46%)
  local copies, waits for them, and re-layouts  71 us (26%)
  other arithmetic  29.3 us (11%)
  between operations  14.2 us (5%)
  blocking collectives  13.7 us (5%)
  matrix products  12.3 us (4%)
  starting transfers between devices  8.61 us (3%)
    reduce_scatter x1, waiting for transfers between devices, body(): lax.psum_scatter((weight_grad * loss_scale).reshape(offsets * channels, c...  124 us
    gather x6, local copies, waits for them, and re-layouts, take_rows(): picked = jnp.take(source, jnp.maximum(row_index, 0), axis=0)  34.5 us
    all_to_all x1, blocking collectives, body(): lax.all_to_all(take_rows(xmask, recv_map, nothing), 'space', split_axis=1...  13.7 us
    select_n x3, other arithmetic, take_rows(): return jnp.where((row_index >= 0)[..., None], picked, nothing)  12.3 us
    select_n x2, local copies, waits for them, and re-layouts, take_rows(): return jnp.where((row_index >= 0)[..., None], picked, nothing)  8.23 us
    all_to_all x1, starting transfers between devices, body(): lax.all_to_all(partial_value, 'space', split_axis=1, concat_axis=1, tiled...  7.28 us
  transfers between devices with their start and end apart: 3, of which 2 were waited for; matrix products, arithmetic and copies ran while one was open for 22% of the time, Pallas kernels for 0%

commit v1 on v0

--- a/solution.py
+++ b/solution.py
@@ -4,6 +4,18 @@
 from jax.sharding import PartitionSpec as P
 
 BLOCK = 128
+
+
+def split_up(x, dim, length):
+    shape = x.shape
+    blocks = x.reshape(*shape[:dim], length, shape[dim] // length, *shape[dim + 1 :])
+    return jnp.moveaxis(blocks, dim, 0)
+
+
+def in_order(pieces, dim):
+    dims = list(pieces.shape[1:])
+    dims[dim] *= pieces.shape[0]
+    return jnp.moveaxis(pieces, 0, dim).reshape(dims)
 
 
 def from_behind(block, axis, distance):
@@ -51,9 +63,15 @@
         .reshape(outgoing.shape)
     )
     arrived = lax.all_to_all(partial_value, "space", split_axis=1, concat_axis=1, tiled=True)
-    returned = lax.all_to_all(
-        take_rows(xmask, recv_map, nothing), "space", split_axis=1, concat_axis=1, tiled=True
-    )
+    x = take_rows(xmask, recv_map, nothing)
+    size, here = (lax.axis_size("space"), lax.axis_index("space"))
+    blocks = split_up(x, 1, size)
+    outs = [blocks[here]]
+    for step in range(1, size):
+        sent = blocks[here ^ step]
+        outs.append(lax.ppermute(sent, "space", [(i_2, i_2 ^ step) for i_2 in range(size)]))
+    blocks = jnp.stack(outs)[here ^ jnp.arange(size)]
+    returned = in_order(blocks, 1)
     weight_grad = weight_grad + lax.dot_general(
         outgoing.reshape(flat_shape),
         returned.reshape(flat_shape),

time: 278 us -> 292 us (1.050)
  blocking collectives: 13.7 us -> 0 us
  starting transfers between devices: 8.61 us -> 20.9 us
  local copies, waits for them, and re-layouts: 71 us -> 79.7 us
  other arithmetic: 29.3 us -> 32.6 us
  waiting for transfers between devices: 127 us -> 130 us
    all_to_all x1 -> x0, blocking collectives: 13.7 us -> none  [body(): lax.all_to_all(take_rows(xmask, recv_map, nothing), 'space', split_axis=1...]
    ppermute x0 -> x7, starting transfers between devices: none -> 12.3 us  [body(): lax.ppermute(sent, 'space', [(i_2, i_2 ^ step) for i_2 in range(size)])]
    unnamed x14 -> x23, local copies, waits for them, and re-layouts: 2.38 us -> 6.79 us
    ppermute x0 -> x7, waiting for transfers between devices: none -> 3.47 us  [body(): lax.ppermute(sent, 'space', [(i_2, i_2 ^ step) for i_2 in range(size)])]
    select_n x2 -> x1, local copies, waits for them, and re-layouts: 8.23 us -> 7.43 us  [take_rows(): return jnp.where((row_index >= 0)[..., None], picked, nothing)]
  transfers between devices with their start and end apart: 3 -> 10, of which waited for: 2 -> 4; matrix products, arithmetic and copies ran while one was open for 22% -> 22% of each run, Pallas kernels for 0% -> 0%
where the time goes in v1:
time: 292 us; the launch traced here: 290 us
  waiting for transfers between devices  130 us (45%)
  local copies, waits for them, and re-layouts  79.7 us (27%)
  other arithmetic  32.6 us (11%)
  starting transfers between devices  20.9 us (7%)
  between operations  14.2 us (5%)
  matrix products  12.3 us (4%)
    reduce_scatter x1, waiting for transfers between devices, body(): lax.psum_scatter((weight_grad * loss_scale).reshape(offsets * channels, c...  125 us
    gather x6, local copies, waits for them, and re-layouts, take_rows(): picked = jnp.take(source, jnp.maximum(row_index, 0), axis=0)  34.4 us
    ppermute x7, starting transfers between devices, body(): lax.ppermute(sent, 'space', [(i_2, i_2 ^ step) for i_2 in range(size)])  12.3 us
    select_n x3, other arithmetic, take_rows(): return jnp.where((row_index >= 0)[..., None], picked, nothing)  11.5 us
    select_n x1, local copies, waits for them, and re-layouts, take_rows(): return jnp.where((row_index >= 0)[..., None], picked, nothing)  7.43 us
    all_to_all x1, starting transfers between devices, body(): lax.all_to_all(partial_value, 'space', split_axis=1, concat_axis=1, tiled...  7.28 us
    unnamed x23, local copies, waits for them, and re-layouts  6.79 us
  transfers between devices with their start and end apart: 10, of which 4 were waited for; matrix products, arithmetic and copies ran while one was open for 22% of the time, Pallas kernels for 0%

profile of v1, /device:TPU:0, one launch (start us, length us, event | category | flops | bytes accessed | tf_op | source)
XLA Modules:
  0.0 289.9 jit_solution(3082822662594912353)
XLA Ops:
  20.7 3.1 %gather_fusion.2 = bf16[432,256]{1,0:T(8,128)(2,1)} fusion(bf16[256,256]{1,0:T(8,128)(2,1)} %bitcast_select_fusion.1, s32[1024]{0:T(1024)S(1)} %get-tuple-element.17), kind=kCustom, calls=%fused_computation.clone | custom fusion | bytes 444096 | tf_op jit(solution)/shard_map/jit(_take)/gather | solution.py:28
  25.5 2.2 broadcast_select_fusion.3
  29.4 2.2 fusion.4
  33.3 1.8 copy.91
  35.1 7.3 %all-to-all-start = ((bf16[27,8,2,256]{3,2,0,1:T(2,128)(2,1)}), bf16[27,8,2,256]{3,2,0,1:T(2,128)(2,1)}, u32[]{:S(2)}, u32[]{:S(2)}) async-start(bf16[27,8,2,256]{3,2,0,1:T(2,128)(2,1)} %copy.91), calls=%async_computation | async-start | bytes 442368 | tf_op jit(solution)/shard_map/all_to_all | solution.py:65
  59.2 18.5 %gather_fusion = bf16[6912,256]{1,0:T(8,128)(2,1)} fusion(bf16[256,256]{1,0:T(8,128)(2,1)} %bitcast_select_fusion.1, s32[7168]{0:T(1024)} %pad_clamp_fusion), kind=kCustom, calls=%fused_computation.2 | custom fusion | bytes 7105536 | tf_op jit(solution)/shard_map/jit(_take)/gather | solution.py:28
  77.6 6.4 %reshape.165 = bf16[256,27,256]{2,1,0:T(8,128)(2,1)} reshape(bf16[6912,256]{1,0:T(8,128)(2,1)} %gather_fusion) | data formatting | bytes 7077888 | tf_op jit(solution)/shard_map/jit(_take)/gather | solution.py:28
  84.0 7.7 %select_select_fusion = bf16[256,27,256]{2,1,0:T(8,128)(2,1)} fusion(bf16[256,27,256]{2,1,0:T(8,128)(2,1)} %reshape.165, pred[256,27]{1,0:T(8,128)(4,1)} %copy.84, pred[256,27]{1,0:T(8,128)(4,1)} %bitcast.90), kind=kLoop, calls=%fused_computation.6 | loop fusion | flops 3538944 | bytes 7091712 | tf_op jit(solution)/shard_map/jit(_where)/select_n | solution.py:29
  91.7 7.4 %copy.94 = bf16[256,27,256]{0,2,1:T(8,128)(2,1)} copy(bf16[256,27,256]{2,1,0:T(8,128)(2,1)} %select_select_fusion) | data formatting | bytes 7077888 | tf_op jit(solution)/shard_map/jit(_where)/select_n | solution.py:29
  99.1 3.8 %fusion.7 = f32[256,256]{1,0:T(8,128)} fusion(bf16[256,27,256]{0,2,1:T(8,128)(2,1)} %copy.94, bf16[1,27,256,256]{3,2,1,0:T(8,128)(2,1)S(1)} %copy-done), kind=kOutput, calls=%fused_computation.12 | convolution fusion | flops 905969664 | bytes 7340032 | tf_op jit(solution)/shard_map/dot_general | solution.py:45
  104.9 2.1 reshape.186
  107.0 4.7 %scatter_fusion = f32[256,256]{1,0:T(8,128)} fusion(f32[256,256]{1,0:T(8,128)} %fusion.7, s32[432]{0:T(512)S(1)} %bitcast.91, f32[432,256]{1,0:T(8,128)} %reshape.186), kind=kCustom, calls=%fused_computation.4 | custom fusion | flops 110592 | bytes 1328832 | tf_op jit(solution)/shard_map/scatter-add | solution.py:83
  111.7 1.8 bitcast_select_fusion
  113.6 3.1 %gather_fusion.3 = bf16[432,256]{1,0:T(8,128)(2,1)} fusion(bf16[256,256]{1,0:T(8,128)(2,1)} %get-tuple-element.14, s32[1024]{0:T(1024)S(1)} %get-tuple-element.16), kind=kCustom, calls=%fused_computation.1.clone | custom fusion | bytes 444096 | tf_op jit(solution)/shard_map/jit(_take)/gather | solution.py:28
  120.1 2.0 collective-permute-start.1
  122.8 3.3 %collective-permute-start.7 = (bf16[27,1,2,256]{3,2,1,0:T(2,128)(2,1)S(1)}, bf16[27,1,2,256]{3,2,1,0:T(2,128)(2,1)S(1)}, u32[]{:S(2)}, u32[]{:S(2)}) collective-permute-start(bf16[27,1,2,256]{3,2,1,0:T(2,128)(2,1)S(1)} %get-tuple-element.7), channel_id=1, source_target_pairs={{0,7},{1,6},{2,5},{3,4},{4,3},{5,2},{6,1},{7,0},{8,15},{9,14},{10,... | collective-permute-start | bytes 82952 | tf_op jit(solution)/shard_map/ppermute | solution.py:72
  126.6 3.3 %collective-permute-start.4 = (bf16[27,1,2,256]{3,2,0,1:T(2,128)(2,1)S(1)}, bf16[27,1,2,256]{3,2,0,1:T(2,128)(2,1)S(1)}, u32[]{:S(2)}, u32[]{:S(2)}) collective-permute-start(bf16[27,1,2,256]{3,2,0,1:T(2,128)(2,1)S(1)} %get-tuple-element.9), channel_id=1, source_target_pairs={{0,4},{1,5},{2,6},{3,7},{4,0},{5,1},{6,2},{7,3},{8,12},{9,13},{10,... | collective-permute-start | bytes 82952 | tf_op jit(solution)/shard_map/ppermute | solution.py:72
  129.9 2.0 collective-permute-start.2
  137.7 2.0 collective-permute-done.6
  140.9 2.7 gather_fusion.1
  147.1 2.3 fusion.12
  149.4 4.0 %add_multiply_fusion = f32[27,256,256]{2,1,0:T(8,128)} fusion(f32[27,256,256]{2,1,0:T(8,128)S(1)} %fusion.12, bf16[256,27,256]{0,2,1:T(8,128)(2,1)S(1)} %copy-done.1, bf16[256,256]{1,0:T(8,128)(2,1)S(1)} %copy-done.2), kind=kOutput, calls=%fused_computation.5 | convolution fusion | flops 909508608 | bytes 17825792 | tf_op jit(solution)/shard_map/dot_general | solution.py:48
  154.7 2.3 collective-permute-done
  157.0 124.5 %reduce-scatter.2.cloned.1.call-done = f32[864,256]{1,0:T(8,128)} async-done(((f32[6912,256]{1,0:T(8,128)}), f32[864,256]{1,0:T(8,128)}) %reduce-scatter.2.cloned.1.call-update) | async-done | bytes 884752 | tf_op jit(solution)/shard_map/reduce_scatter | solution.py:87
  (74 shorter events, 55.3 us)
Async XLA Ops:
  7.2 22.3 %copy-start = (bf16[1,27,256,256]{3,2,1,0:T(8,128)(2,1)S(1)}, bf16[1,27,256,256]{3,2,1,0:T(8,128)(2,1)}, u32[]{:S(2)}) copy-start(bf16[1,27,256,256]{3,2,1,0:T(8,128)(2,1)} %param.11) | copy-start | bytes 10616836
  23.8 19.3 %copy-start.4 = (s32[1,1,27,8,2]{2,4,3,1,0:T(2,128)S(1)}, s32[1,1,27,8,2]{2,4,3,1,0:T(2,128)}, u32[]{:S(2)}) copy-start(s32[1,1,27,8,2]{2,4,3,1,0:T(2,128)} %param.15) | copy-start | bytes 5188
  23.8 26.2 %copy-start.5 = (pred[27,8,2]{0,2,1:T(4,128)(4,1)S(1)}, pred[27,8,2]{0,2,1:T(4,128)(4,1)}, u32[]{:S(2)}) copy-start(pred[27,8,2]{0,2,1:T(4,128)(4,1)} %get-tuple-element.3) | copy-start | bytes 1300
  35.1 67.8 %all-to-all-start = ((bf16[27,8,2,256]{3,2,0,1:T(2,128)(2,1)}), bf16[27,8,2,256]{3,2,0,1:T(2,128)(2,1)}, u32[]{:S(2)}, u32[]{:S(2)}) async-start(bf16[27,8,2,256]{3,2,0,1:T(2,128)(2,1)} %copy.91), calls=%async_computation | async-start | bytes 442368 | tf_op jit(solution)/shard_map/all_to_all | solution.py:65
  42.4 239.1 %reduce-scatter.2.cloned.1.call-start = ((), (), s32[]{:S(2)}) async-start(), calls=%async_computation.2 | async-start | bytes 7962624 | tf_op jit(solution)/shard_map/reduce_scatter | solution.py:87
  44.4 1.4 copy-start.3
  107.0 4.7 %copy-start.6 = (pred[256]{0:T(512)(128)(4,1)S(1)}, pred[256]{0:T(512)(128)(4,1)}, u32[]{:S(2)}) copy-start(pred[256]{0:T(512)(128)(4,1)} %compare_bitcast_fusion.2) | copy-start | bytes 772
  120.1 9.7 %collective-permute-start.1 = (bf16[27,1,2,256]{3,2,0,1:T(2,128)(2,1)S(1)}, bf16[27,1,2,256]{3,2,0,1:T(2,128)(2,1)S(1)}, u32[]{:S(2)}, u32[]{:S(2)}) collective-permute-start(bf16[27,1,2,256]{3,2,0,1:T(2,128)(2,1)S(1)} %get-tuple-element.12), channel_id=1, source_target_pairs={{0,1},{1,0},{2,3},{3,2},{4,5},{5,4},{6,7},{7,6},{8,9},{9,8},{10,11... | collective-permute-start | bytes 82952 | tf_op jit(solution)/shard_map/ppermute | solution.py:72
  122.8 17.5 %collective-permute-start.7 = (bf16[27,1,2,256]{3,2,1,0:T(2,128)(2,1)S(1)}, bf16[27,1,2,256]{3,2,1,0:T(2,128)(2,1)S(1)}, u32[]{:S(2)}, u32[]{:S(2)}) collective-permute-start(bf16[27,1,2,256]{3,2,1,0:T(2,128)(2,1)S(1)} %get-tuple-element.7), channel_id=1, source_target_pairs={{0,7},{1,6},{2,5},{3,4},{4,3},{5,2},{6,1},{7,0},{8,15},{9,14},{10,... | collective-permute-start | bytes 82952 | tf_op jit(solution)/shard_map/ppermute | solution.py:72
  126.0 11.1 %collective-permute-start.5 = (bf16[27,1,2,256]{3,2,0,1:T(2,128)(2,1)S(1)}, bf16[27,1,2,256]{3,2,0,1:T(2,128)(2,1)S(1)}, u32[]{:S(2)}, u32[]{:S(2)}) collective-permute-start(bf16[27,1,2,256]{3,2,0,1:T(2,128)(2,1)S(1)} %get-tuple-element.8), channel_id=1, source_target_pairs={{0,5},{1,4},{2,7},{3,6},{4,1},{5,0},{6,3},{7,2},{8,13},{9,12},{10,... | collective-permute-start | bytes 82952 | tf_op jit(solution)/shard_map/ppermute | solution.py:72
  126.6 9.9 %collective-permute-start.4 = (bf16[27,1,2,256]{3,2,0,1:T(2,128)(2,1)S(1)}, bf16[27,1,2,256]{3,2,0,1:T(2,128)(2,1)S(1)}, u32[]{:S(2)}, u32[]{:S(2)}) collective-permute-start(bf16[27,1,2,256]{3,2,0,1:T(2,128)(2,1)S(1)} %get-tuple-element.9), channel_id=1, source_target_pairs={{0,4},{1,5},{2,6},{3,7},{4,0},{5,1},{6,2},{7,3},{8,12},{9,13},{10,... | collective-permute-start | bytes 82952 | tf_op jit(solution)/shard_map/ppermute | solution.py:72
  129.8 6.0 %collective-permute-start.3 = (bf16[27,1,2,256]{3,2,0,1:T(2,128)(2,1)S(1)}, bf16[27,1,2,256]{3,2,0,1:T(2,128)(2,1)S(1)}, u32[]{:S(2)}, u32[]{:S(2)}) collective-permute-start(bf16[27,1,2,256]{3,2,0,1:T(2,128)(2,1)S(1)} %get-tuple-element.10), channel_id=1, source_target_pairs={{0,3},{1,2},{2,1},{3,0},{4,7},{5,6},{6,5},{7,4},{8,11},{9,10},{10,... | collective-permute-start | bytes 82952 | tf_op jit(solution)/shard_map/ppermute | solution.py:72
  129.9 4.2 %collective-permute-start.2 = (bf16[27,1,2,256]{3,2,0,1:T(2,128)(2,1)S(1)}, bf16[27,1,2,256]{3,2,0,1:T(2,128)(2,1)S(1)}, u32[]{:S(2)}, u32[]{:S(2)}) collective-permute-start(bf16[27,1,2,256]{3,2,0,1:T(2,128)(2,1)S(1)} %get-tuple-element.11), channel_id=1, source_target_pairs={{0,2},{1,3},{2,0},{3,1},{4,6},{5,7},{6,4},{7,5},{8,10},{9,11},{10,... | collective-permute-start | bytes 82952 | tf_op jit(solution)/shard_map/ppermute | solution.py:72
  134.0 5.7 %collective-permute-start.6 = (bf16[27,1,2,256]{3,2,0,1:T(2,128)(2,1)S(1)}, bf16[27,1,2,256]{3,2,0,1:T(2,128)(2,1)S(1)}, u32[]{:S(2)}, u32[]{:S(2)}) collective-permute-start(bf16[27,1,2,256]{3,2,0,1:T(2,128)(2,1)S(1)} %get-tuple-element.13), channel_id=1, source_target_pairs={{0,6},{1,7},{2,4},{3,5},{4,2},{5,3},{6,0},{7,1},{8,14},{9,15},{10,... | collective-permute-start | bytes 82952 | tf_op jit(solution)/shard_map/ppermute | solution.py:72
  147.1 2.3 copy-start.1
  147.1 2.3 copy-start.2
  153.4 3.6 %collective-permute-start = (bf16[256,256]{1,0:T(8,128)(2,1)}, bf16[256,256]{1,0:T(8,128)(2,1)}, u32[]{:S(2)}, u32[]{:S(2)}) collective-permute-start(bf16[256,256]{1,0:T(8,128)(2,1)} %get-tuple-element.15), channel_id=1, source_target_pairs={{8,0},{16,8},{24,16},{9,1},{17,9},{25,17},{10,2},{18,10},{26,18},{... | collective-permute-start | bytes 393224 | tf_op jit(solution)/shard_map/ppermute | solution.py:24
Sparse Core Ops, SparseCore 0:
  153.5 127.9 reduce-scatter.1
